TPU v7x, 32 devices: a whole 2x2x4 slice. The times are simulated.
32 devices in a mesh: fsdp: 8 (over z, y), seq: 4 (over x, core).
Axes of the slice: x: 2, y: 2, z: 4, core: 2. Of those that a mesh axis runs over, the one named last changes fastest.
Arguments:
- activations: bfloat16 [8, 2560, 1024], P('fsdp', 'seq'), may hold values from -6 to 6
- cotangent: bfloat16 [8, 2560, 1024], P('fsdp', 'seq'), may hold values from -6 to 6
- gain_attn: bfloat16 [1024], P('fsdp'), may hold values from 0.25 to 1.75
- w_qkv: bfloat16 [1024, 3072], P('fsdp'), may hold values from -0.25 to 0.25
- w_attn_out: bfloat16 [1024, 1024], P('fsdp'), may hold values from -0.75 to 0.75
- gain_mlp: bfloat16 [1024], P('fsdp'), may hold values from 0.25 to 1.75
- w_in: bfloat16 [1024, 5248], P('fsdp'), may hold values from -0.1875 to 0.1875
- w_mlp_out: bfloat16 [2624, 1024], P('fsdp'), may hold values from -0.125 to 0.125
Outputs:
- output: bfloat16 [8, 2560, 1024], P('fsdp', 'seq')
- d_input: bfloat16 [8, 2560, 1024], P('fsdp', 'seq')
- grad_gain_attn: float32 [1024], P('fsdp')
- grad_gain_mlp: float32 [1024], P('fsdp')
- grad_w_qkv: float32 [1024, 3072], P('fsdp')
- grad_w_attn_out: float32 [1024, 1024], P('fsdp')
- grad_w_in: float32 [1024, 5248], P('fsdp')
- grad_w_mlp_out: float32 [2624, 1024], P('fsdp')
All inputs are finite; a program needn't handle non-finite values.
Results may differ from a plain program's by a relative error of at most 0.023.
Values may be sent and summed in bfloat16 or wider, within the bound.
No kernel may reach another device: no remote copies, remote signals or barrier semaphores. Data moves between devices by JAX's collectives and lax.ppermute only.
A program may use at most 192 MiB of HBM per device.

v0:
```python
import math
import jax
import jax.numpy as jnp
from jax import lax
from jax.sharding import PartitionSpec as P

HEADS = 16
HEAD = 64
FF = 2624
LENGTH = 2560
QB = 512
eps = 1e-05
rope_base = 160000.0


def layer_norm(values, gain_vec):
    average = jnp.mean(values, -1, keepdims=True)
    centred = values - average
    variance = jnp.mean(centred * centred, -1, keepdims=True)
    return centred * lax.rsqrt(variance + eps) * gain_vec


def gelu_exact(values):
    return 0.5 * values * (1.0 + lax.erf(values * 2.0 ** (-0.5)))


def rope_tables(positions):
    half_size = HEAD // 2
    freq_index = jnp.arange(half_size).astype(positions.dtype)
    inverse = jnp.exp(freq_index * (-2.0 * math.log(rope_base) / HEAD))
    angles = positions[:, None] * inverse[None, :]
    angles = jnp.concatenate([angles, angles], 1)
    return (jnp.cos(angles), jnp.sin(angles))


def rotate(tensor, cosine, sine_table):
    half_size = HEAD // 2
    first = tensor[..., :half_size]
    second = tensor[..., half_size:]
    turned = jnp.concatenate([-second, first], -1)
    return tensor * cosine + turned * sine_table


def contract_rows(left, right):
    return lax.dot_general(
        left, right, (((0,), (0,)), ((), ())), preferred_element_type=jnp.float32
    )


def times_transpose(left, right):
    return lax.dot_general(
        left, right, (((1,), (1,)), ((), ())), preferred_element_type=jnp.float32
    )


def split_heads(packed_heads):
    local_heads = packed_heads.shape[2] // HEAD
    queries = packed_heads[:, 0].reshape(LENGTH // QB, QB, local_heads, HEAD)
    key_rows = packed_heads[:, 1].reshape(LENGTH, local_heads, HEAD)
    value_rows = packed_heads[:, 2].reshape(LENGTH, local_heads, HEAD)
    return (local_heads, queries, key_rows, value_rows)


def attend_sequence(packed_heads):
    local_heads, queries, key_rows, value_rows = split_heads(packed_heads)
    factor = float(HEAD) ** (-0.5)

    def one_block(q_block):
        scores = (
            jnp.einsum("qhd,khd->hqk", q_block, key_rows, preferred_element_type=jnp.float32)
            * factor
        )
        row_peak = jnp.max(scores, -1, keepdims=True)
        exponent = jnp.exp(scores - row_peak)
        row_total = jnp.sum(exponent, -1, keepdims=True)
        probs = (exponent / row_total).astype(jnp.bfloat16)
        attended = jnp.einsum("hqk,khd->qhd", probs, value_rows, preferred_element_type=jnp.float32)
        attended = attended.astype(jnp.bfloat16).reshape(QB, local_heads * HEAD)
        return (attended, (row_peak + jnp.log(row_total))[..., 0])

    attended, log_sums = lax.map(one_block, queries)
    return (attended.reshape(LENGTH, local_heads * HEAD), log_sums)


def attend_backward(pieces):
    packed_heads, log_sums, grad_heads = pieces
    local_heads, queries, key_rows, value_rows = split_heads(packed_heads)
    factor = float(HEAD) ** (-0.5)
    grad_blocks = grad_heads.reshape(LENGTH // QB, QB, local_heads, HEAD)

    def one_block(carry, block_pieces):
        key_grad, value_grad = carry
        q_block, lse_block, g_block = block_pieces
        scores = (
            jnp.einsum("qhd,khd->hqk", q_block, key_rows, preferred_element_type=jnp.float32)
            * factor
        )
        probs = jnp.exp(scores - lse_block[..., None])
        value_grad = value_grad + jnp.einsum(
            "hqk,qhd->khd", probs.astype(jnp.bfloat16), g_block, preferred_element_type=jnp.float32
        )
        prob_grad = jnp.einsum(
            "qhd,khd->hqk", g_block, value_rows, preferred_element_type=jnp.float32
        )
        inner = jnp.sum(probs * prob_grad, -1, keepdims=True)
        score_grad = (probs * (prob_grad - inner)).astype(jnp.bfloat16)
        query_grad = (
            jnp.einsum("hqk,khd->qhd", score_grad, key_rows, preferred_element_type=jnp.float32)
            * factor
        )
        key_grad = (
            key_grad
            + jnp.einsum("hqk,qhd->khd", score_grad, q_block, preferred_element_type=jnp.float32)
            * factor
        )
        return ((key_grad, value_grad), query_grad)

    zeros_state = jnp.zeros((LENGTH, local_heads, HEAD), jnp.float32)
    (key_grad, value_grad), query_grad = lax.scan(
        one_block, (zeros_state, zeros_state), (queries, log_sums, grad_blocks)
    )
    width_local = local_heads * HEAD
    stacked = jnp.stack(
        [
            query_grad.reshape(LENGTH, width_local),
            key_grad.reshape(LENGTH, width_local),
            value_grad.reshape(LENGTH, width_local),
        ],
        1,
    )
    return stacked.astype(jnp.bfloat16)


def local(activations, cotangent, gain_attn, w_qkv, w_attn_out, gain_mlp, w_in, w_mlp_out):
    local_seqs, positions, width = activations.shape
    row_count = local_seqs * positions
    gathered = (
        lax.all_gather(gain_attn, "fsdp", axis=0, tiled=True),
        lax.all_gather(w_qkv, "fsdp", axis=0, tiled=True),
        lax.all_gather(w_attn_out, "fsdp", axis=0, tiled=True),
        lax.all_gather(gain_mlp, "fsdp", axis=0, tiled=True),
        lax.all_gather(w_in, "fsdp", axis=0, tiled=True),
        lax.all_gather(w_mlp_out, "fsdp", axis=0, tiled=True),
    )
    full_gain_attn, full_qkv, full_attn_out, full_gain_mlp, full_in, full_mlp_out = gathered
    tokens = activations.astype(jnp.float32).reshape(row_count, width)
    normed, first_back = jax.vjp(layer_norm, tokens, full_gain_attn.astype(jnp.float32))
    normed_low = normed.astype(jnp.bfloat16)
    packed = jnp.dot(normed_low, full_qkv, preferred_element_type=jnp.float32)
    packed = packed.reshape(local_seqs, positions, 3, HEADS, HEAD)
    starting = (lax.axis_index("seq") * positions).astype(jnp.float32)
    places = starting + jnp.arange(positions).astype(jnp.float32)
    cosine, sine_table = rope_tables(places)

    def turn_pair(pair_values):
        return rotate(pair_values, cosine[:, None, None, :], sine_table[:, None, None, :])

    turned, turn_back = jax.vjp(turn_pair, packed[:, :, :2])
    rotated = jnp.concatenate([turned, packed[:, :, 2:]], 2).astype(jnp.bfloat16)
    rotated = rotated.reshape(local_seqs, positions, 3, width)
    heads_layout = lax.all_to_all(rotated, "seq", split_axis=3, concat_axis=1, tiled=True)
    attended_heads, log_sums = lax.map(attend_sequence, heads_layout)
    attended = lax.all_to_all(attended_heads, "seq", split_axis=1, concat_axis=2, tiled=True)
    attended_rows = attended.reshape(row_count, width)
    mixed = tokens + jnp.dot(attended_rows, full_attn_out, preferred_element_type=jnp.float32)
    normed_mlp, norm_back = jax.vjp(layer_norm, mixed, full_gain_mlp.astype(jnp.float32))
    normed_mlp_low = normed_mlp.astype(jnp.bfloat16)
    gate_up = jnp.dot(normed_mlp_low, full_in, preferred_element_type=jnp.float32)

    def gated(gate_part, up_part):
        return gelu_exact(gate_part) * up_part

    hidden, gated_back = jax.vjp(gated, gate_up[:, :FF], gate_up[:, FF:])
    hidden_low = hidden.astype(jnp.bfloat16)
    result = mixed + jnp.dot(hidden_low, full_mlp_out, preferred_element_type=jnp.float32)
    output = result.astype(jnp.bfloat16).reshape(activations.shape)
    again = (
        lax.all_gather(w_qkv, "fsdp", axis=0, tiled=True),
        lax.all_gather(w_attn_out, "fsdp", axis=0, tiled=True),
        lax.all_gather(w_in, "fsdp", axis=0, tiled=True),
        lax.all_gather(w_mlp_out, "fsdp", axis=0, tiled=True),
    )
    again_qkv, again_attn_out, again_in, again_mlp_out = again
    out_grad = cotangent.reshape(row_count, width)
    grad_mlp_out = contract_rows(hidden_low, out_grad)
    hidden_grad = times_transpose(out_grad, again_mlp_out)
    gate_grad, up_grad = gated_back(hidden_grad)
    gate_up_grad = jnp.concatenate([gate_grad, up_grad], 1).astype(jnp.bfloat16)
    grad_in = contract_rows(normed_mlp_low, gate_up_grad)
    normed_mlp_grad = times_transpose(gate_up_grad, again_in)
    mixed_grad_norm, grad_gain_mlp = norm_back(normed_mlp_grad)
    mixed_grad = out_grad.astype(jnp.float32) + mixed_grad_norm
    mixed_low = mixed_grad.astype(jnp.bfloat16)
    grad_attn_out = contract_rows(attended_rows, mixed_low)
    attended_grad = times_transpose(mixed_low, again_attn_out).astype(jnp.bfloat16)
    attended_grad = attended_grad.reshape(local_seqs, positions, width)
    grad_heads = lax.all_to_all(attended_grad, "seq", split_axis=2, concat_axis=1, tiled=True)
    rotated_grad = lax.map(attend_backward, (heads_layout, log_sums, grad_heads))
    position_grad = lax.all_to_all(rotated_grad, "seq", split_axis=1, concat_axis=3, tiled=True)
    position_grad = position_grad.astype(jnp.float32).reshape(local_seqs, positions, 3, HEADS, HEAD)
    (pair_grad,) = turn_back(position_grad[:, :, :2])
    packed_grad = jnp.concatenate([pair_grad, position_grad[:, :, 2:]], 2).astype(jnp.bfloat16)
    packed_grad = packed_grad.reshape(row_count, 3 * width)
    grad_qkv = contract_rows(normed_low, packed_grad)
    normed_grad = times_transpose(packed_grad, again_qkv)
    token_grad_norm, grad_gain_attn = first_back(normed_grad)
    d_input = (mixed_grad + token_grad_norm).astype(jnp.bfloat16).reshape(activations.shape)
    gradients = (grad_gain_attn, grad_gain_mlp, grad_qkv, grad_attn_out, grad_in, grad_mlp_out)
    shards = (
        lax.psum_scatter(
            gradients[0].astype(jnp.bfloat16), "fsdp", scatter_dimension=0, tiled=True
        ).astype(jnp.float32),
        lax.psum_scatter(
            gradients[1].astype(jnp.bfloat16), "fsdp", scatter_dimension=0, tiled=True
        ).astype(jnp.float32),
        lax.psum_scatter(
            gradients[2].astype(jnp.bfloat16), "fsdp", scatter_dimension=0, tiled=True
        ).astype(jnp.float32),
        lax.psum_scatter(
            gradients[3].astype(jnp.bfloat16), "fsdp", scatter_dimension=0, tiled=True
        ).astype(jnp.float32),
        lax.psum_scatter(
            gradients[4].astype(jnp.bfloat16), "fsdp", scatter_dimension=0, tiled=True
        ).astype(jnp.float32),
        lax.psum_scatter(
            gradients[5].astype(jnp.bfloat16), "fsdp", scatter_dimension=0, tiled=True
        ).astype(jnp.float32),
    )
    shards = (
        lax.psum(shards[0].astype(jnp.bfloat16), "seq").astype(jnp.float32),
        lax.psum(shards[1].astype(jnp.bfloat16), "seq").astype(jnp.float32),
        lax.psum(shards[2].astype(jnp.bfloat16), "seq").astype(jnp.float32),
        lax.psum(shards[3].astype(jnp.bfloat16), "seq").astype(jnp.float32),
        lax.psum(shards[4].astype(jnp.bfloat16), "seq").astype(jnp.float32),
        lax.psum(shards[5].astype(jnp.bfloat16), "seq").astype(jnp.float32),
    )
    return (output, d_input, shards[0], shards[1], shards[2], shards[3], shards[4], shards[5])


def solution(mesh):
    in_specs = (
        P("fsdp", "seq", None),
        P("fsdp", "seq", None),
        P("fsdp"),
        P("fsdp", None),
        P("fsdp", None),
        P("fsdp"),
        P("fsdp", None),
        P("fsdp", None),
    )
    out_specs = (
        P("fsdp", "seq", None),
        P("fsdp", "seq", None),
        P("fsdp"),
        P("fsdp"),
        P("fsdp", None),
        P("fsdp", None),
        P("fsdp", None),
        P("fsdp", None),
    )
    return jax.shard_map(local, mesh=mesh, in_specs=in_specs, out_specs=out_specs, check_vma=False)
```

profile of v0, /device:TPU:0, one launch (start us, length us, event | category | flops | bytes accessed | tf_op | source)
XLA Modules:
  0.0 1313.2 jit_solution(7243004674187600519)
XLA Ops:
  9.4 22.5 %all-gather = bf16[8,1,128]{2,1,0:T(2,128)(2,1)S(1)} all-gather(bf16[1,1,128]{2,1,0:T(2,128)(2,1)} %bitcast.228), channel_id=1, replica_groups=mesh['fsdp'=8,'seq'=4] {'fsdp'}, dimensions={0}, use_global_device_ids=true | all-gather | bytes 2304 | tf_op jit(solution)/shard_map/all_gather | solution.py:138
  33.7 78.3 %all-gather.7.cloned.1.call-done = bf16[1024,3072]{1,0:T(8,128)(2,1)} async-done(((bf16[128,3072]{1,0:T(8,128)(2,1)}), bf16[1024,3072]{1,0:T(8,128)(2,1)}) %all-gather.7.cloned.1.call-update) | async-done | bytes 6291472 | tf_op jit(solution)/shard_map/all_gather | solution.py:139
  112.0 8.7 copy.50
  120.6 7.9 convolution_bitcast_fusion
  134.9 6.5 pad_maximum_fusion.1
  147.1 58.9 %all-to-all-done = bf16[1,640,3,1024]{1,2,0,3:T(4,128)(2,1)} async-done(((bf16[1,640,3,1024]{1,2,0,3:T(4,128)(2,1)}), bf16[1,640,3,1024]{1,2,0,3:T(4,128)(2,1)}, u32[]{:S(2)}, u32[]{:S(2)}) %all-to-all-start) | async-done | bytes 3932192 | tf_op jit(solution)/shard_map/all_to_all | solution.py:161
  206.0 8.2 copy.53
  214.1 7.4 squeeze.44
  228.4 93.1 %while.45 = (s32[]{:T(128)}, bf16[5,512,256]{2,1,0:T(8,128)(2,1)}, f32[5,4,512]{2,1,0:T(4,128)}, bf16[5,512,4,64]{1,3,2,0:T(8,128)(2,1)}, bf16[2560,4,64]{0,2,1:...) while((s32[]{:T(128)}, bf16[5,512,256]{2,1,0:T(8,128)(2,1)}, f32[5,4,512]{2,1,0:T(4,128)}, ...), condition=%wide.region_5.0_spmd, body=%wide.region_2.5_spmd.sunk | while | flops 1389492224 | bytes 67174496 | solution.py:81
  237.9 6.6 fusion.120
  256.5 6.7 fusion.120
  275.1 6.6 fusion.120
  293.9 6.6 fusion.120
  312.5 6.6 fusion.120
  326.2 14.1 %reduce.1 = bf16[2560,256]{1,0:T(8,128)(2,1)} reduce(bf16[2560,1,256]{2,1,0:T(2,128)(2,1)S(1)} %bitcast.202, bf16[]{:T(256)} %broadcast.257), dimensions={1}, to_apply=%bitcast.158.reduce_sub_computation | reduce | bytes 2621442
  347.5 17.7 %all-gather.1 = bf16[8,1,128]{2,1,0:T(2,128)(2,1)S(1)} all-gather(bf16[1,1,128]{2,1,0:T(2,128)(2,1)S(1)} %bitcast.229), channel_id=1, replica_groups=mesh['fsdp'=8,'seq'=4] {'fsdp'}, dimensions={0}, use_global_device_ids=true | all-gather | bytes 2304 | tf_op jit(solution)/shard_map/all_gather | solution.py:141
  377.1 15.1 %fusion.73 = f32[640,5248]{1,0:T(8,128)} fusion(bf16[1024,5248]{1,0:T(8,128)(2,1)} %all-gather.11.cloned.1.call-done, f32[640,1024]{1,0:T(8,128)} %copy-done.7, f32[1024]{0:T(1024)S(1)} %bitcast.224, f32[640]{0:T(1024)S(1)} %fusion.67, f32[640]{0:T(1024)S(1)} %broadcast_multiply_fusion.1), kind=kOutput, calls=%fused_computation.125 | convolution fusion | flops 6881280000 | bytes 26813440 | tf_op jit(solution)/shard_map/dot_general | solution.py:168
  392.1 12.3 all-gather.13.cloned.1.call-done
  404.5 14.9 %add_convert_fusion = (bf16[640,2624]{1,0:T(8,128)(2,1)S(1)}, bf16[640,2624]{1,0:T(8,128)(2,1)}, bf16[640,2624]{1,0:T(8,128)(2,1)}) fusion(f32[640,5248]{1,0:T(8,128)} %fusion.73, bf16[2624,1024]{1,0:T(8,128)(2,1)} %all-gather.13.cloned.1.call-done, bf16[1,640,1024]{2,1,0:T(8,128)(2,1)} %param.13), kind=kOutput, calls=%fused_computation.48 | convolution fusion | flops 3471237120 | bytes 30195712 | tf_op jit(solution)/shard_map/dot_general | solution.py:51
  419.4 14.6 %multiply_reduce_fusion.2 = (bf16[1024]{0:T(1024)(128)(2,1)}, f32[640]{0:T(1024)S(1)}, f32[640,1024]{1,0:T(8,128)S(1)}) fusion(f32[640,1024]{1,0:T(8,128)S(1)} %copy-done.8, f32[640]{0:T(1024)S(1)} %fusion.67, f32[640]{0:T(1024)S(1)} %broadcast_multiply_fusion.1, f32[1024]{0:T(1024)S(1)} %bitcast.225, bf16[1024,5248]{1,0:T(8,128)(2,1)} %all-gather.11.cloned.1.call-done, ...), kind=kOutput, calls=%fused_computation.88 | convolution fusion | flops 6896679424 | bytes 22722048 | tf_op jit(solution)/shard_map/dot_general | solution.py:51
  443.1 5.4 copy.60
  448.4 9.7 reduce.2
  466.2 8.3 convolution_convert_fusion.1
  474.6 8.9 all-to-all-done.2
  490.0 323.5 %while.46 = (s32[]{:T(128)}, f32[2560,4,64]{0,2,1:T(8,128)}, f32[2560,4,64]{0,2,1:T(8,128)}, bf16[5,512,4,64]{1,3,2,0:T(8,128)(2,1)}, bf16[5,512,4,64]{1,3,2,0:T...) while((s32[]{:T(128)}, f32[2560,4,64]{0,2,1:T(8,128)}, ...), condition=%wide.region_12.13_spmd.clone, body=%wide.region_10.12_spmd.clone.sunk | while | flops 3421763584 | bytes 173334672 | solution.py:119
  490.9 11.4 fusion.130
  502.2 12.6 fusion.132
  514.8 14.7 %multiply_reduce_fusion.8 = (f32[4,512]{1,0:T(4,128)S(1)}, f32[4,512,2560]{2,1,0:T(8,128)}) fusion(f32[4,512,2560]{2,1,0:T(8,128)} %fusion.130, f32[4,512]{1,0:T(4,128)S(1)} %dynamic-slice_bitcast_fusion.2, bf16[2560,4,64]{0,2,1:T(8,128)(2,1)} %get-tuple-element.413, bf16[5,512,4,64]{1,3,2,0:T(8,128)(2,1)} %get-tuple-element.412, s32[]{:T(128)S(6)} %copy.94), kind=kOutput, calls=%fused_computation.14.clone.1 | convolution fusion | flops 692058112 | bytes 43532292 | tf_op jit(solution)/shard_map/while/body/eval_jaxpr/while/body/eval_jaxpr/qhd,khd->hqk/dot_general | solution.py:102
  529.5 15.1 %multiply_convert_fusion.7 = bf16[4,512,2560]{2,1,0:T(8,128)(2,1)S(1)} fusion(f32[4,512,2560]{2,1,0:T(8,128)} %get-tuple-element.360, f32[4,512,2560]{2,1,0:T(8,128)} %fusion.130, f32[4,512]{1,0:T(4,128)S(1)} %get-tuple-element.361, f32[4,512]{1,0:T(4,128)S(1)} %dynamic-slice_bitcast_fusion.2), kind=kLoop, calls=%fused_computation.13.clone.1 | loop fusion | flops 26214400 | bytes 52445184 | tf_op jit(solution)/shard_map/while/body/eval_jaxpr/while/body/eval_jaxpr/convert_element_type | solution.py:106
  555.1 11.5 fusion.130
  566.6 13.6 %fusion.132 = f32[2560,4,64]{0,2,1:T(8,128)} fusion(f32[4,512,2560]{2,1,0:T(8,128)} %fusion.130, f32[4,512]{1,0:T(4,128)S(1)} %dynamic-slice_bitcast_fusion.2, f32[2560,4,64]{0,2,1:T(8,128)} %get-tuple-element.396, pred[]{:T(512)S(6)} %compare.5, bf16[5,512,4,64]{1,3,2,0:T(8,128)(2,1)} %get-tuple-element.412, s32[]{:T(128)S(6)} %copy.94), kind=kOutput, calls=%fused_computation.24.clone.1 | convolution fusion | flops 688128000 | bytes 26484740 | tf_op jit(solution)/shard_map/while/body/eval_jaxpr/while/body/eval_jaxpr/hqk,qhd->khd/dot_general | solution.py:99
  580.2 14.3 %multiply_reduce_fusion.8 = (f32[4,512]{1,0:T(4,128)S(1)}, f32[4,512,2560]{2,1,0:T(8,128)}) fusion(f32[4,512,2560]{2,1,0:T(8,128)} %fusion.130, f32[4,512]{1,0:T(4,128)S(1)} %dynamic-slice_bitcast_fusion.2, bf16[2560,4,64]{0,2,1:T(8,128)(2,1)} %get-tuple-element.413, bf16[5,512,4,64]{1,3,2,0:T(8,128)(2,1)} %get-tuple-element.412, s32[]{:T(128)S(6)} %copy.94), kind=kOutput, calls=%fused_computation.14.clone.1 | convolution fusion | flops 692058112 | bytes 43532292 | tf_op jit(solution)/shard_map/while/body/eval_jaxpr/while/body/eval_jaxpr/qhd,khd->hqk/dot_general | solution.py:102
  594.4 14.7 %multiply_convert_fusion.7 = bf16[4,512,2560]{2,1,0:T(8,128)(2,1)S(1)} fusion(f32[4,512,2560]{2,1,0:T(8,128)} %get-tuple-element.360, f32[4,512,2560]{2,1,0:T(8,128)} %fusion.130, f32[4,512]{1,0:T(4,128)S(1)} %get-tuple-element.361, f32[4,512]{1,0:T(4,128)S(1)} %dynamic-slice_bitcast_fusion.2), kind=kLoop, calls=%fused_computation.13.clone.1 | loop fusion | flops 26214400 | bytes 52445184 | tf_op jit(solution)/shard_map/while/body/eval_jaxpr/while/body/eval_jaxpr/convert_element_type | solution.py:106
  609.2 5.3 fusion.133
  614.5 5.3 fusion.131
  620.5 11.3 fusion.130
  631.8 13.3 %fusion.132 = f32[2560,4,64]{0,2,1:T(8,128)} fusion(f32[4,512,2560]{2,1,0:T(8,128)} %fusion.130, f32[4,512]{1,0:T(4,128)S(1)} %dynamic-slice_bitcast_fusion.2, f32[2560,4,64]{0,2,1:T(8,128)} %get-tuple-element.396, pred[]{:T(512)S(6)} %compare.5, bf16[5,512,4,64]{1,3,2,0:T(8,128)(2,1)} %get-tuple-element.412, s32[]{:T(128)S(6)} %copy.94), kind=kOutput, calls=%fused_computation.24.clone.1 | convolution fusion | flops 688128000 | bytes 26484740 | tf_op jit(solution)/shard_map/while/body/eval_jaxpr/while/body/eval_jaxpr/hqk,qhd->khd/dot_general | solution.py:99
  645.1 14.2 %multiply_reduce_fusion.8 = (f32[4,512]{1,0:T(4,128)S(1)}, f32[4,512,2560]{2,1,0:T(8,128)}) fusion(f32[4,512,2560]{2,1,0:T(8,128)} %fusion.130, f32[4,512]{1,0:T(4,128)S(1)} %dynamic-slice_bitcast_fusion.2, bf16[2560,4,64]{0,2,1:T(8,128)(2,1)} %get-tuple-element.413, bf16[5,512,4,64]{1,3,2,0:T(8,128)(2,1)} %get-tuple-element.412, s32[]{:T(128)S(6)} %copy.94), kind=kOutput, calls=%fused_computation.14.clone.1 | convolution fusion | flops 692058112 | bytes 43532292 | tf_op jit(solution)/shard_map/while/body/eval_jaxpr/while/body/eval_jaxpr/qhd,khd->hqk/dot_general | solution.py:102
  659.3 14.3 %multiply_convert_fusion.7 = bf16[4,512,2560]{2,1,0:T(8,128)(2,1)S(1)} fusion(f32[4,512,2560]{2,1,0:T(8,128)} %get-tuple-element.360, f32[4,512,2560]{2,1,0:T(8,128)} %fusion.130, f32[4,512]{1,0:T(4,128)S(1)} %get-tuple-element.361, f32[4,512]{1,0:T(4,128)S(1)} %dynamic-slice_bitcast_fusion.2), kind=kLoop, calls=%fused_computation.13.clone.1 | loop fusion | flops 26214400 | bytes 52445184 | tf_op jit(solution)/shard_map/while/body/eval_jaxpr/while/body/eval_jaxpr/convert_element_type | solution.py:106
  679.0 5.3 fusion.131
  685.0 11.3 fusion.130
  696.3 13.3 %fusion.132 = f32[2560,4,64]{0,2,1:T(8,128)} fusion(f32[4,512,2560]{2,1,0:T(8,128)} %fusion.130, f32[4,512]{1,0:T(4,128)S(1)} %dynamic-slice_bitcast_fusion.2, f32[2560,4,64]{0,2,1:T(8,128)} %get-tuple-element.396, pred[]{:T(512)S(6)} %compare.5, bf16[5,512,4,64]{1,3,2,0:T(8,128)(2,1)} %get-tuple-element.412, s32[]{:T(128)S(6)} %copy.94), kind=kOutput, calls=%fused_computation.24.clone.1 | convolution fusion | flops 688128000 | bytes 26484740 | tf_op jit(solution)/shard_map/while/body/eval_jaxpr/while/body/eval_jaxpr/hqk,qhd->khd/dot_general | solution.py:99
  709.6 14.2 %multiply_reduce_fusion.8 = (f32[4,512]{1,0:T(4,128)S(1)}, f32[4,512,2560]{2,1,0:T(8,128)}) fusion(f32[4,512,2560]{2,1,0:T(8,128)} %fusion.130, f32[4,512]{1,0:T(4,128)S(1)} %dynamic-slice_bitcast_fusion.2, bf16[2560,4,64]{0,2,1:T(8,128)(2,1)} %get-tuple-element.413, bf16[5,512,4,64]{1,3,2,0:T(8,128)(2,1)} %get-tuple-element.412, s32[]{:T(128)S(6)} %copy.94), kind=kOutput, calls=%fused_computation.14.clone.1 | convolution fusion | flops 692058112 | bytes 43532292 | tf_op jit(solution)/shard_map/while/body/eval_jaxpr/while/body/eval_jaxpr/qhd,khd->hqk/dot_general | solution.py:102
  723.8 14.3 %multiply_convert_fusion.7 = bf16[4,512,2560]{2,1,0:T(8,128)(2,1)S(1)} fusion(f32[4,512,2560]{2,1,0:T(8,128)} %get-tuple-element.360, f32[4,512,2560]{2,1,0:T(8,128)} %fusion.130, f32[4,512]{1,0:T(4,128)S(1)} %get-tuple-element.361, f32[4,512]{1,0:T(4,128)S(1)} %dynamic-slice_bitcast_fusion.2), kind=kLoop, calls=%fused_computation.13.clone.1 | loop fusion | flops 26214400 | bytes 52445184 | tf_op jit(solution)/shard_map/while/body/eval_jaxpr/while/body/eval_jaxpr/convert_element_type | solution.py:106
  738.1 5.3 fusion.133
  743.5 5.3 fusion.131
  749.5 11.3 fusion.130
  760.8 13.3 %fusion.132 = f32[2560,4,64]{0,2,1:T(8,128)} fusion(f32[4,512,2560]{2,1,0:T(8,128)} %fusion.130, f32[4,512]{1,0:T(4,128)S(1)} %dynamic-slice_bitcast_fusion.2, f32[2560,4,64]{0,2,1:T(8,128)} %get-tuple-element.396, pred[]{:T(512)S(6)} %compare.5, bf16[5,512,4,64]{1,3,2,0:T(8,128)(2,1)} %get-tuple-element.412, s32[]{:T(128)S(6)} %copy.94), kind=kOutput, calls=%fused_computation.24.clone.1 | convolution fusion | flops 688128000 | bytes 26484740 | tf_op jit(solution)/shard_map/while/body/eval_jaxpr/while/body/eval_jaxpr/hqk,qhd->khd/dot_general | solution.py:99
  774.1 14.2 %multiply_reduce_fusion.8 = (f32[4,512]{1,0:T(4,128)S(1)}, f32[4,512,2560]{2,1,0:T(8,128)}) fusion(f32[4,512,2560]{2,1,0:T(8,128)} %fusion.130, f32[4,512]{1,0:T(4,128)S(1)} %dynamic-slice_bitcast_fusion.2, bf16[2560,4,64]{0,2,1:T(8,128)(2,1)} %get-tuple-element.413, bf16[5,512,4,64]{1,3,2,0:T(8,128)(2,1)} %get-tuple-element.412, s32[]{:T(128)S(6)} %copy.94), kind=kOutput, calls=%fused_computation.14.clone.1 | convolution fusion | flops 692058112 | bytes 43532292 | tf_op jit(solution)/shard_map/while/body/eval_jaxpr/while/body/eval_jaxpr/qhd,khd->hqk/dot_general | solution.py:102
  788.3 14.3 %multiply_convert_fusion.7 = bf16[4,512,2560]{2,1,0:T(8,128)(2,1)S(1)} fusion(f32[4,512,2560]{2,1,0:T(8,128)} %get-tuple-element.360, f32[4,512,2560]{2,1,0:T(8,128)} %fusion.130, f32[4,512]{1,0:T(4,128)S(1)} %get-tuple-element.361, f32[4,512]{1,0:T(4,128)S(1)} %dynamic-slice_bitcast_fusion.2), kind=kLoop, calls=%fused_computation.13.clone.1 | loop fusion | flops 26214400 | bytes 52445184 | tf_op jit(solution)/shard_map/while/body/eval_jaxpr/while/body/eval_jaxpr/convert_element_type | solution.py:106
  802.6 5.3 fusion.133
  807.9 5.3 fusion.131
  825.6 8.6 copy.65
  834.2 63.3 %all_to_all.54 = bf16[1,2560,3,256]{3,2,0,1:T(4,128)(2,1)S(1)} all-to-all(bf16[1,2560,3,256]{3,2,0,1:T(4,128)(2,1)} %copy.65), channel_id=1, replica_groups=mesh['fsdp'=8,'seq'=4] {'seq'}, dimensions={1} | all-to-all | bytes 7864320 | tf_op jit(solution)/shard_map/all_to_all | solution.py:199
  901.9 9.2 copy.67
  920.8 7.8 convolution_convert_fusion.2
  929.3 15.7 %convolution_convert_fusion = bf16[1024,5248]{1,0:T(8,128)(2,1)} fusion(bf16[640,2624]{1,0:T(8,128)(2,1)} %get-tuple-element.246, bf16[640,2624]{1,0:T(8,128)(2,1)} %copy-done.41, f32[640,1024]{1,0:T(8,128)} %copy-done.7, f32[1024]{0:T(1024)S(1)} %bitcast.227, f32[640]{0:T(1024)S(1)} %copy-done.36, f32[640]{0:T(1024)S(1)} %copy-done.24), kind=kOutput, calls=%fused_computation.44 | convolution fusion | flops 6900088832 | bytes 20096000 | tf_op jit(solution)/shard_map/dot_general | solution.py:45
  946.9 9.4 fusion.57
  956.3 88.0 %reduce-scatter.5.cloned.1.call-done = bf16[128,3072]{1,0:T(8,128)(2,1)} async-done(((bf16[1024,3072]{1,0:T(8,128)(2,1)}), bf16[128,3072]{1,0:T(8,128)(2,1)}) %reduce-scatter.5.cloned.1.call-update) | async-done | bytes 786448 | tf_op jit(solution)/shard_map/reduce_scatter | solution.py:216
  1044.3 185.0 %reduce-scatter.9.cloned.1.call-done = bf16[128,5248]{1,0:T(8,128)(2,1)} async-done(((bf16[1024,5248]{1,0:T(8,128)(2,1)}), bf16[128,5248]{1,0:T(8,128)(2,1)}) %reduce-scatter.9.cloned.1.call-update) | async-done | bytes 1343504 | tf_op jit(solution)/shard_map/reduce_scatter | solution.py:222
  1229.3 8.1 fusion.49
  1238.9 19.6 %all-reduce.4 = (bf16[1024]{0:T(1024)(128)(2,1)S(1)}, bf16[1024]{0:T(1024)(128)(2,1)S(1)}) all-reduce(bf16[1024]{0:T(1024)(128)(2,1)S(1)} %get-tuple-element.199, bf16[1024]{0:T(1024)(128)(2,1)S(1)} %copy-done.37), channel_id=2, replica_groups=mesh['fsdp'=8,'seq'=4] {'fsdp'}, use_global_device_ids=true, to_apply=%region_16.17.clone | all-reduce | flops 2048 | bytes 8192
  1258.7 6.0 all-reduce.5
  1269.7 29.3 %all-reduce.9.cloned.1.call-done = (bf16[128,3072]{1,0:T(8,128)(2,1)}, bf16[128,1024]{1,0:T(8,128)(2,1)}, bf16[128,5248]{1,0:T(8,128)(2,1)}, bf16[328,1024]{1,0:T(8,128)(2,1)}) async-done(((bf16[128,3072]{1,0:T(8,128)(2,1)}, bf16[128,1024]{1,0:T(8,128)(2,1)}, bf16[128,5248]{1,0:T(8,128)(2,1)}, bf16[328,1024]{1,0:T(8,128)(2,1)}), (bf16[128,3072]{1,0:T(8,128)(2,1)}, bf16[128,1024]{1,0:T(8,128)(2,1)}, ...) | async-done | bytes 3063824 | tf_op jit(solution)/shard_map/psum | solution.py:232
  (218 shorter events, 190.2 us)
Async XLA Ops:
  7.2 25.2 %copy-start.3 = (bf16[1,640,1024]{2,1,0:T(8,128)(2,1)S(1)}, bf16[1,640,1024]{2,1,0:T(8,128)(2,1)}, u32[]{:S(2)}) copy-start(bf16[1,640,1024]{2,1,0:T(8,128)(2,1)} %param.12) | copy-start | bytes 3932164
  7.2 104.8 %all-gather.7.cloned.1.call-start = ((), (), s32[]{:S(2)}) async-start(), calls=%async_computation.8 | async-start | bytes 7077888 | tf_op jit(solution)/shard_map/all_gather | solution.py:139
  7.9 363.6 %all-gather.9.cloned.1.call-start = ((), (), s32[]{:S(2)}) async-start(), calls=%async_computation.9 | async-start | bytes 2359296 | tf_op jit(solution)/shard_map/all_gather | solution.py:140
  8.7 368.4 %all-gather.11.cloned.1.call-start = ((), (), s32[]{:S(2)}) async-start(), calls=%async_computation.10 | async-start | bytes 12091392 | tf_op jit(solution)/shard_map/all_gather | solution.py:142
  31.9 88.7 %copy-start.27 = (f32[8,1,128]{2,1,0:T(1,128)}, f32[8,1,128]{2,1,0:T(1,128)S(1)}, u32[]{:S(2)}) copy-start(f32[8,1,128]{2,1,0:T(1,128)S(1)} %convert_element_type.213) | copy-start | bytes 12292
  32.3 98.8 %copy-start.14 = (f32[640,64]{0,1:T(8,128)}, f32[640,64]{0,1:T(8,128)S(1)}, u32[]{:S(2)}) copy-start(f32[640,64]{0,1:T(8,128)S(1)} %get-tuple-element.255) | copy-start | bytes 491524
  32.4 98.8 %copy-start.16 = (f32[640,64]{0,1:T(8,128)}, f32[640,64]{0,1:T(8,128)S(1)}, u32[]{:S(2)}) copy-start(f32[640,64]{0,1:T(8,128)S(1)} %get-tuple-element.256) | copy-start | bytes 491524
  32.6 88.0 %copy-start.21 = (f32[640]{0:T(1024)}, f32[640]{0:T(1024)S(1)}, u32[]{:S(2)}) copy-start(f32[640]{0:T(1024)S(1)} %broadcast_multiply_fusion.2) | copy-start | bytes 7684
  33.1 0.6 copy-start.25
  33.7 87.0 %copy-start.29 = (f32[640]{0:T(1024)}, f32[640]{0:T(1024)S(1)}, u32[]{:S(2)}) copy-start(f32[640]{0:T(1024)S(1)} %fusion.66) | copy-start | bytes 7684
  141.4 64.5 %all-to-all-start = ((bf16[1,640,3,1024]{1,2,0,3:T(4,128)(2,1)}), bf16[1,640,3,1024]{1,2,0,3:T(4,128)(2,1)}, u32[]{:S(2)}, u32[]{:S(2)}) async-start(bf16[1,640,3,1024]{1,2,0,3:T(4,128)(2,1)} %pad_maximum_fusion.1), calls=%async_computation | async-start | bytes 10485760 | tf_op jit(solution)/shard_map/all_to_all | solution.py:161
  146.5 258.0 %all-gather.13.cloned.1.call-start = ((), (), s32[]{:S(2)}) async-start(), calls=%async_computation.11 | async-start | bytes 6045696 | tf_op jit(solution)/shard_map/all_gather | solution.py:143
  340.3 7.2 copy-start.38
  343.9 21.3 %all-to-all-start.1 = ((bf16[4,2,81920]{2,1,0:T(2,128)(2,1)}), bf16[4,2,81920]{2,1,0:T(2,128)(2,1)S(1)}, u32[]{:S(2)}, u32[]{:S(2)}) async-start(bf16[4,2,81920]{2,1,0:T(2,128)(2,1)} %reshape.443), calls=%async_computation.1 | async-start | bytes 2621440 | tf_op jit(solution)/shard_map/all_to_all | solution.py:163
  347.5 608.8 %reduce-scatter.7.cloned.1.call-start = ((), (), s32[]{:S(2)}) async-start(), calls=%async_computation.13 | async-start | bytes 2359296 | tf_op jit(solution)/shard_map/reduce_scatter | solution.py:219
  365.2 68.8 %copy-start.33 = (f32[8,1,128]{2,1,0:T(1,128)}, f32[8,1,128]{2,1,0:T(1,128)S(1)}, u32[]{:S(2)}) copy-start(f32[8,1,128]{2,1,0:T(1,128)S(1)} %convert_element_type.214) | copy-start | bytes 12292
  368.0 3.5 copy-start.4
  375.1 1.5 copy-start.7
  375.2 58.9 %copy-start.23 = (f32[640]{0:T(1024)}, f32[640]{0:T(1024)S(1)}, u32[]{:S(2)}) copy-start(f32[640]{0:T(1024)S(1)} %broadcast_multiply_fusion.1) | copy-start | bytes 7684
  377.0 57.1 %copy-start.35 = (f32[640]{0:T(1024)}, f32[640]{0:T(1024)S(1)}, u32[]{:S(2)}) copy-start(f32[640]{0:T(1024)S(1)} %fusion.67) | copy-start | bytes 7684
  392.1 27.3 %copy-start.8 = (f32[640,1024]{1,0:T(8,128)S(1)}, f32[640,1024]{1,0:T(8,128)}, u32[]{:S(2)}) copy-start(f32[640,1024]{1,0:T(8,128)} %copy-done.7) | copy-start | bytes 7864324
  419.4 14.6 %copy-start.41 = (bf16[640,2624]{1,0:T(8,128)(2,1)}, bf16[640,2624]{1,0:T(8,128)(2,1)S(1)}, u32[]{:S(2)}) copy-start(bf16[640,2624]{1,0:T(8,128)(2,1)S(1)} %get-tuple-element.245) | copy-start | bytes 10076164
  434.1 1.3 copy-start.11
  435.0 1.5 copy-start.1
  435.0 1.5 copy-start.31
  435.4 1.8 copy-start.19
  437.2 3.2 copy-start.39
  458.1 8.1 copy-start.12
  461.8 21.6 %all-to-all-start.2 = ((bf16[4,2,81920]{2,1,0:T(2,128)(2,1)}), bf16[4,2,81920]{2,1,0:T(2,128)(2,1)}, u32[]{:S(2)}, u32[]{:S(2)}) async-start(bf16[4,2,81920]{2,1,0:T(2,128)(2,1)} %reshape.445), calls=%async_computation.2 | async-start | bytes 2621440 | tf_op jit(solution)/shard_map/all_to_all | solution.py:197
  466.2 490.1 %reduce-scatter.11.cloned.1.call-start = ((), (), s32[]{:S(2)}) async-start(), calls=%async_computation.15 | async-start | bytes 6045696 | tf_op jit(solution)/shard_map/reduce_scatter | solution.py:225
  474.5 569.8 %reduce-scatter.5.cloned.1.call-start = ((), (), s32[]{:S(2)}) async-start(), calls=%async_computation.12 | async-start | bytes 7077888 | tf_op jit(solution)/shard_map/reduce_scatter | solution.py:216
  813.5 7.7 copy-start
  821.3 2.1 copy-start.10
  911.1 2.1 copy-start.17
  911.1 5.5 slice-start
  913.2 3.9 slice-start.1
  916.2 1.1 copy-start.15
  918.5 2.3 copy-start.5
  918.5 2.3 copy-start.22
  918.5 2.3 copy-start.28
  918.5 2.3 copy-start.30
  918.9 1.9 copy-start.13
  928.6 0.7 copy-start.24
  928.6 0.7 copy-start.34
  928.6 0.7 copy-start.36
  928.7 300.6 %reduce-scatter.9.cloned.1.call-start = ((), (), s32[]{:S(2)}) async-start(), calls=%async_computation.14 | async-start | bytes 12091392 | tf_op jit(solution)/shard_map/reduce_scatter | solution.py:222
  945.0 0.7 copy-start.40
  945.0 353.9 %all-reduce.9.cloned.1.call-start = ((), (), s32[]{:S(2)}) async-start(), calls=%async_computation.16 | async-start | bytes 6127616 | tf_op jit(solution)/shard_map/psum | solution.py:232
  1229.3 8.2 copy-start.26
  1229.3 8.2 copy-start.6
  1237.4 1.5 copy-start.9
  1237.4 1.5 copy-start.37
  1237.5 28.3 %copy-start.2 = (f32[640,1024]{1,0:T(8,128)S(1)}, f32[640,1024]{1,0:T(8,128)}, u32[]{:S(2)}) copy-start(f32[640,1024]{1,0:T(8,128)} %copy-done.1) | copy-start | bytes 7864324
  1237.5 28.2 %copy-start.32 = (f32[640]{0:T(1024)S(1)}, f32[640]{0:T(1024)}, u32[]{:S(2)}) copy-start(f32[640]{0:T(1024)} %copy-done.31) | copy-start | bytes 7684
  1299.0 4.4 copy-start.20
  1299.0 5.6 copy-start.18
Sparse Core Ops, SparseCore 0:
  10.2 101.7 all-gather.6
  114.1 47.4 all-gather.8
  163.8 152.5 all-gather.10
  318.4 86.0 all-gather.12
  440.6 66.1 reduce-scatter.6
  510.2 103.5 reduce-scatter.10
  928.8 115.4 reduce-scatter.4
  1048.3 180.8 reduce-scatter.8
  1231.9 67.0 all-reduce.8
where the time goes:
time: 1320 us; the launch traced here: 1310 us
  waiting for transfers between devices  463 us (35%)
  matrix products  413 us (31%)
  other arithmetic  163 us (12%)
  blocking collectives  129 us (10%)
  local copies, waits for them, and re-layouts  116 us (9%)
  between operations  15.6 us (1%)
  starting transfers between devices  13.6 us (1%)
    reduce_scatter x1, waiting for transfers between devices, local(): lax.psum_scatter(gradients[4].astype(jnp.bfloat16), 'fsdp', scatter_dimen...  185 us
    reduce_scatter x1, waiting for transfers between devices, local(): lax.psum_scatter(gradients[2].astype(jnp.bfloat16), 'fsdp', scatter_dimen...  88 us
    dot_general x10, matrix products, one_block(): jnp.einsum('qhd,khd->hqk', q_block, key_rows, preferred_element_type=jnp....  79 us
    all_gather x1, waiting for transfers between devices, local(): lax.all_gather(w_qkv, 'fsdp', axis=0, tiled=True)  78.3 us
    convert_element_type x5, other arithmetic, one_block(): score_grad = (probs * (prob_grad - inner)).astype(jnp.bfloat16)  72.9 us
    dot_general x5, matrix products, one_block(): jnp.einsum('qhd,khd->hqk', g_block, value_rows, preferred_element_type=jn...  71.4 us
    dot_general x5, matrix products, one_block(): jnp.einsum('hqk,qhd->khd', probs.astype(jnp.bfloat16), g_block, preferred...  66 us
    all_to_all x1, blocking collectives, local(): lax.all_to_all(rotated_grad, 'seq', split_axis=1, concat_axis=3, tiled=True)  63.3 us
  transfers between devices with their start and end apart: 12, of which 7 were waited for; matrix products, arithmetic and copies ran while one was open for 49% of the time, Pallas kernels for 0%

commit v1 on v0

--- a/solution.py
+++ b/solution.py
@@ -11,6 +11,18 @@
 QB = 512
 eps = 1e-05
 rope_base = 160000.0
+
+
+def doubled_up(array, axis, dim):
+    ways, here = (lax.axis_size(axis), lax.axis_index(axis))
+    grown, reach = (array, 1)
+    while reach < ways:
+        theirs = lax.ppermute(grown, axis, [(d, d ^ reach) for d in range(ways)])
+        mine_first = jnp.concatenate([grown, theirs], axis=dim)
+        theirs_first = jnp.concatenate([theirs, grown], axis=dim)
+        grown = jnp.where(here & reach == 0, mine_first, theirs_first)
+        reach = 2 * reach
+    return grown
 
 
 def layer_norm(values, gain_vec):
@@ -136,7 +148,7 @@
     row_count = local_seqs * positions
     gathered = (
         lax.all_gather(gain_attn, "fsdp", axis=0, tiled=True),
-        lax.all_gather(w_qkv, "fsdp", axis=0, tiled=True),
+        doubled_up(w_qkv, "fsdp", 0),
         lax.all_gather(w_attn_out, "fsdp", axis=0, tiled=True),
         lax.all_gather(gain_mlp, "fsdp", axis=0, tiled=True),
         lax.all_gather(w_in, "fsdp", axis=0, tiled=True),

time: 1320 us -> 1650 us (1.25)
  waiting for transfers between devices: 463 us -> 698 us
  blocking collectives: 129 us -> 220 us
    ppermute x0 -> x3, waiting for transfers between devices: none -> 226 us  [doubled_up(): theirs = lax.ppermute(grown, axis, [(d, d ^ reach) for d in range(ways)])]
    all_gather x1, blocking collectives: 22.5 us -> 105 us  [local(): lax.all_gather(gain_attn, 'fsdp', axis=0, tiled=True)]
    all_gather x1, waiting for transfers between devices: 78.3 us -> 100 us  [local(): lax.all_gather(w_qkv, 'fsdp', axis=0, tiled=True)]
  transfers between devices with their start and end apart: 12 -> 15, of which waited for: 7 -> 9; matrix products, arithmetic and copies ran while one was open for 49% -> 39% of each run, Pallas kernels for 0% -> 0%
where the time goes in v1:
time: 1650 us
  waiting for transfers between devices  698 us (42%)
  matrix products  411 us (25%)
  blocking collectives  220 us (13%)
  other arithmetic  177 us (11%)
  local copies, waits for them, and re-layouts  107 us (6%)
  starting transfers between devices  20.5 us (1%)
    ppermute x3, waiting for transfers between devices, doubled_up(): theirs = lax.ppermute(grown, axis, [(d, d ^ reach) for d in range(ways)])  226 us
    reduce_scatter x1, waiting for transfers between devices, local(): lax.psum_scatter(gradients[4].astype(jnp.bfloat16), 'fsdp', scatter_dimen...  185 us
    all_gather x1, blocking collectives, local(): lax.all_gather(gain_attn, 'fsdp', axis=0, tiled=True)  105 us
    all_gather x1, waiting for transfers between devices, local(): lax.all_gather(w_qkv, 'fsdp', axis=0, tiled=True)  100 us
    reduce_scatter x1, waiting for transfers between devices, local(): lax.psum_scatter(gradients[2].astype(jnp.bfloat16), 'fsdp', scatter_dimen...  87.7 us
    dot_general x10, matrix products, one_block(): jnp.einsum('qhd,khd->hqk', q_block, key_rows, preferred_element_type=jnp....  79.1 us
    convert_element_type x5, other arithmetic, one_block(): score_grad = (probs * (prob_grad - inner)).astype(jnp.bfloat16)  72.9 us
    dot_general x5, matrix products, one_block(): jnp.einsum('qhd,khd->hqk', g_block, value_rows, preferred_element_type=jn...  71.7 us
  transfers between devices with their start and end apart: 15, of which 9 were waited for; matrix products, arithmetic and copies ran while one was open for 39% of the time, Pallas kernels for 0%

profile of v1, /device:TPU:0, one launch (start us, length us, event | category | flops | bytes accessed | tf_op | source)
XLA Modules:
  0.0 1649.5 jit_solution(17928021364418721769)
XLA Ops:
  13.2 20.5 %collective-permute-done = bf16[128,3072]{0,1:T(8,128)(2,1)} collective-permute-done((bf16[128,3072]{0,1:T(8,128)(2,1)S(1)}, bf16[128,3072]{0,1:T(8,128)(2,1)}, u32[]{:S(2)}, u32[]{:S(2)}) %collective-permute-start) | collective-permute-done | bytes 786464 | tf_op jit(solution)/shard_map/ppermute | solution.py:20
  37.4 50.9 %collective-permute-done.1 = bf16[256,3072]{0,1:T(8,128)(2,1)} collective-permute-done((bf16[256,3072]{0,1:T(8,128)(2,1)S(1)}, bf16[256,3072]{0,1:T(8,128)(2,1)}, u32[]{:S(2)}, u32[]{:S(2)}) %collective-permute-start.1) | collective-permute-done | bytes 1572896 | tf_op jit(solution)/shard_map/ppermute | solution.py:20
  94.5 104.8 %all-gather = bf16[8,1,128]{2,1,0:T(2,128)(2,1)S(1)} all-gather(bf16[1,1,128]{2,1,0:T(2,128)(2,1)S(1)} %bitcast.228), channel_id=1, replica_groups=mesh['fsdp'=8,'seq'=4] {'fsdp'}, dimensions={0}, use_global_device_ids=true | all-gather | bytes 2304 | tf_op jit(solution)/shard_map/all_gather | solution.py:150
  200.5 154.3 %collective-permute-done.2 = bf16[512,3072]{0,1:T(8,128)(2,1)} collective-permute-done((bf16[512,3072]{0,1:T(8,128)(2,1)}, bf16[512,3072]{0,1:T(8,128)(2,1)}, u32[]{:S(2)}, u32[]{:S(2)}) %collective-permute-start.2) | collective-permute-done | bytes 3145760 | tf_op jit(solution)/shard_map/ppermute | solution.py:20
  354.8 7.7 maximum_select_fusion
  362.6 5.3 convolution_bitcast_fusion
  374.3 7.0 pad_maximum_fusion.1
  387.2 58.7 %all-to-all-done = bf16[1,640,3,1024]{1,2,0,3:T(4,128)(2,1)} async-done(((bf16[1,640,3,1024]{1,2,0,3:T(4,128)(2,1)}), bf16[1,640,3,1024]{1,2,0,3:T(4,128)(2,1)}, u32[]{:S(2)}, u32[]{:S(2)}) %all-to-all-start) | async-done | bytes 3932192 | tf_op jit(solution)/shard_map/all_to_all | solution.py:173
  445.9 8.2 copy.59
  454.0 7.4 squeeze.44
  468.3 93.1 %while.45 = (s32[]{:T(128)}, bf16[5,512,256]{2,1,0:T(8,128)(2,1)}, f32[5,4,512]{2,1,0:T(4,128)}, bf16[5,512,4,64]{1,3,2,0:T(8,128)(2,1)}, bf16[2560,4,64]{0,2,1:...) while((s32[]{:T(128)}, bf16[5,512,256]{2,1,0:T(8,128)(2,1)}, f32[5,4,512]{2,1,0:T(4,128)}, ...), condition=%wide.region_5.6_spmd, body=%wide.region_2.5_spmd.sunk | while | flops 1389492224 | bytes 67174496 | solution.py:93
  478.0 6.6 fusion.120
  496.6 6.6 fusion.120
  515.2 6.6 fusion.120
  533.8 6.6 fusion.120
  552.4 6.6 fusion.120
  566.0 14.1 reduce.1
  587.4 27.0 %all-gather.1 = bf16[8,1,128]{2,1,0:T(2,128)(2,1)S(1)} all-gather(bf16[1,1,128]{2,1,0:T(2,128)(2,1)S(1)} %bitcast.229), channel_id=1, replica_groups=mesh['fsdp'=8,'seq'=4] {'fsdp'}, dimensions={0}, use_global_device_ids=true | all-gather | bytes 2304 | tf_op jit(solution)/shard_map/all_gather | solution.py:153
  626.2 15.0 fusion.73
  641.3 15.2 add_convert_fusion
  656.5 14.6 multiply_reduce_fusion.2
  680.0 5.4 copy.66
  685.4 9.7 reduce.2
  703.2 8.2 convolution_convert_fusion.1
  711.5 8.9 all-to-all-done.2
  726.9 323.7 %while.46 = (s32[]{:T(128)}, f32[2560,4,64]{0,2,1:T(8,128)}, f32[2560,4,64]{0,2,1:T(8,128)}, bf16[5,512,4,64]{1,3,2,0:T(8,128)(2,1)}, bf16[5,512,4,64]{1,3,2,0:T...) while((s32[]{:T(128)}, f32[2560,4,64]{0,2,1:T(8,128)}, ...), condition=%wide.region_12.13_spmd.clone, body=%wide.region_10.12_spmd.clone.sunk | while | flops 3421763584 | bytes 173334672 | solution.py:131
  727.8 11.5 fusion.130
  739.3 12.5 fusion.132
  751.8 14.7 multiply_reduce_fusion.8
  766.5 15.1 multiply_convert_fusion.7
  781.6 5.3 fusion.133
  792.1 11.5 fusion.130
  803.6 13.6 fusion.132
  817.2 14.3 multiply_reduce_fusion.8
  831.5 14.7 multiply_convert_fusion.7
  851.5 5.4 fusion.131
  857.6 11.3 fusion.130
  868.9 13.2 fusion.132
  882.1 14.3 multiply_reduce_fusion.8
  896.4 14.3 multiply_convert_fusion.7
  916.0 5.4 fusion.131
  922.1 11.3 fusion.130
  933.4 13.2 fusion.132
  946.6 14.2 multiply_reduce_fusion.8
  960.9 14.3 multiply_convert_fusion.7
  980.5 5.4 fusion.131
  986.6 11.3 fusion.130
  997.9 13.2 fusion.132
  1011.1 14.2 multiply_reduce_fusion.8
  1025.4 14.3 multiply_convert_fusion.7
  1045.0 5.4 fusion.131
  1062.7 8.7 copy.71
  1071.4 63.3 %all_to_all.54 = bf16[1,2560,3,256]{3,2,0,1:T(4,128)(2,1)S(1)} all-to-all(bf16[1,2560,3,256]{3,2,0,1:T(4,128)(2,1)} %copy.71), channel_id=1, replica_groups=mesh['fsdp'=8,'seq'=4] {'seq'}, dimensions={1} | all-to-all | bytes 7864320 | tf_op jit(solution)/shard_map/all_to_all | solution.py:211
  1139.0 9.1 copy.73
  1158.0 7.7 convolution_convert_fusion.2
  1166.4 15.7 convolution_convert_fusion
  1184.1 9.4 fusion.57
  1193.6 87.7 %reduce-scatter.5.cloned.1.call-done = bf16[128,3072]{1,0:T(8,128)(2,1)} async-done(((bf16[1024,3072]{1,0:T(8,128)(2,1)}), bf16[128,3072]{1,0:T(8,128)(2,1)}) %reduce-scatter.5.cloned.1.call-update) | async-done | bytes 786448 | tf_op jit(solution)/shard_map/reduce_scatter | solution.py:228
  1281.2 184.9 %reduce-scatter.9.cloned.1.call-done = bf16[128,5248]{1,0:T(8,128)(2,1)} async-done(((bf16[1024,5248]{1,0:T(8,128)(2,1)}), bf16[128,5248]{1,0:T(8,128)(2,1)}) %reduce-scatter.9.cloned.1.call-update) | async-done | bytes 1343504 | tf_op jit(solution)/shard_map/reduce_scatter | solution.py:234
  1466.2 100.3 %all-gather.13.cloned.1.call-done = bf16[1024,3072]{1,0:T(8,128)(2,1)} async-done(((bf16[128,3072]{1,0:T(8,128)(2,1)}), bf16[1024,3072]{1,0:T(8,128)(2,1)}) %all-gather.13.cloned.1.call-update) | async-done | bytes 6291472 | tf_op jit(solution)/shard_map/all_gather | solution.py:190
  1566.5 8.1 fusion.49
  1576.1 18.7 %all-reduce.4 = (bf16[1024]{0:T(1024)(128)(2,1)S(1)}, bf16[1024]{0:T(1024)(128)(2,1)S(1)}) all-reduce(bf16[1024]{0:T(1024)(128)(2,1)S(1)} %get-tuple-element.199, bf16[1024]{0:T(1024)(128)(2,1)S(1)} %copy-done.37), channel_id=2, replica_groups=mesh['fsdp'=8,'seq'=4] {'fsdp'}, use_global_device_ids=true, to_apply=%region_16.17.clone | all-reduce | flops 2048 | bytes 8192
  1595.0 6.0 all-reduce.5
  1606.0 29.3 %all-reduce.9.cloned.1.call-done = (bf16[128,3072]{1,0:T(8,128)(2,1)}, bf16[128,1024]{1,0:T(8,128)(2,1)}, bf16[128,5248]{1,0:T(8,128)(2,1)}, bf16[328,1024]{1,0:T(8,128)(2,1)}) async-done(((bf16[128,3072]{1,0:T(8,128)(2,1)}, bf16[128,1024]{1,0:T(8,128)(2,1)}, bf16[128,5248]{1,0:T(8,128)(2,1)}, bf16[328,1024]{1,0:T(8,128)(2,1)}), (bf16[128,3072]{1,0:T(8,128)(2,1)}, bf16[128,1024]{1,0:T(8,128)(2,1)}, ...) | async-done | bytes 3063824 | tf_op jit(solution)/shard_map/psum | solution.py:244
  (229 shorter events, 214.4 us)
Async XLA Ops:
  7.2 613.5 %all-gather.7.cloned.1.call-start = ((), (), s32[]{:S(2)}) async-start(), calls=%async_computation.8 | async-start | bytes 2359296 | tf_op jit(solution)/shard_map/all_gather | solution.py:152
  7.9 618.3 %all-gather.9.cloned.1.call-start = ((), (), s32[]{:S(2)}) async-start(), calls=%async_computation.9 | async-start | bytes 12091392 | tf_op jit(solution)/shard_map/all_gather | solution.py:154
  10.2 23.5 %collective-permute-start = (bf16[128,3072]{0,1:T(8,128)(2,1)S(1)}, bf16[128,3072]{0,1:T(8,128)(2,1)}, u32[]{:S(2)}, u32[]{:S(2)}) collective-permute-start(bf16[128,3072]{0,1:T(8,128)(2,1)S(1)} %copy.55), channel_id=1, source_target_pairs={{0,4},{4,0},{8,12},{12,8},{16,20},{20,16},{24,28},{28,24},{1,5},{5... | collective-permute-start | bytes 2359304 | tf_op jit(solution)/shard_map/ppermute | solution.py:20
  35.6 52.8 %collective-permute-start.1 = (bf16[256,3072]{0,1:T(8,128)(2,1)S(1)}, bf16[256,3072]{0,1:T(8,128)(2,1)}, u32[]{:S(2)}, u32[]{:S(2)}) collective-permute-start(bf16[256,3072]{0,1:T(8,128)(2,1)S(1)} %maximum_select_fusion.2), channel_id=1, source_target_pairs={{0,8},{4,12},{8,0},{12,4},{16,24},{20,28},{24,16},{28,20},{1,9},{5... | collective-permute-start | bytes 4718600 | tf_op jit(solution)/shard_map/ppermute | solution.py:20
  37.4 57.1 %copy-start.38 = (bf16[128]{0:T(256)(128)(2,1)S(1)}, bf16[128]{0:T(256)(128)(2,1)}, u32[]{:S(2)}) copy-start(bf16[128]{0:T(256)(128)(2,1)} %param.14) | copy-start | bytes 772
  37.4 162.3 %copy-start.3 = (bf16[1,640,1024]{2,1,0:T(8,128)(2,1)S(1)}, bf16[1,640,1024]{2,1,0:T(8,128)(2,1)}, u32[]{:S(2)}) copy-start(bf16[1,640,1024]{2,1,0:T(8,128)(2,1)} %param.12) | copy-start | bytes 3932164
  92.2 262.6 %collective-permute-start.2 = (bf16[512,3072]{0,1:T(8,128)(2,1)}, bf16[512,3072]{0,1:T(8,128)(2,1)}, u32[]{:S(2)}, u32[]{:S(2)}) collective-permute-start(bf16[512,3072]{0,1:T(8,128)(2,1)} %maximum_select_fusion.1), channel_id=1, source_target_pairs={{0,16},{4,20},{8,24},{12,28},{16,0},{20,4},{24,8},{28,12},{1,17},{... | collective-permute-start | bytes 9437192 | tf_op jit(solution)/shard_map/ppermute | solution.py:20
  199.3 163.2 %copy-start.27 = (f32[8,1,128]{2,1,0:T(1,128)}, f32[8,1,128]{2,1,0:T(1,128)S(1)}, u32[]{:S(2)}) copy-start(f32[8,1,128]{2,1,0:T(1,128)S(1)} %convert_element_type.213) | copy-start | bytes 12292
  199.7 170.8 %copy-start.14 = (f32[640,64]{0,1:T(8,128)}, f32[640,64]{0,1:T(8,128)S(1)}, u32[]{:S(2)}) copy-start(f32[640,64]{0,1:T(8,128)S(1)} %get-tuple-element.255) | copy-start | bytes 491524
  199.8 170.8 %copy-start.16 = (f32[640,64]{0,1:T(8,128)}, f32[640,64]{0,1:T(8,128)S(1)}, u32[]{:S(2)}) copy-start(f32[640,64]{0,1:T(8,128)S(1)} %get-tuple-element.256) | copy-start | bytes 491524
  200.0 162.6 %copy-start.21 = (f32[640]{0:T(1024)}, f32[640]{0:T(1024)S(1)}, u32[]{:S(2)}) copy-start(f32[640]{0:T(1024)S(1)} %broadcast_multiply_fusion.2) | copy-start | bytes 7684
  200.5 162.1 %copy-start.25 = (f32[640]{0:T(1024)}, f32[640]{0:T(1024)S(1)}, u32[]{:S(2)}) copy-start(f32[640]{0:T(1024)S(1)} %fusion.48) | copy-start | bytes 7684
  200.5 162.1 %copy-start.29 = (f32[640]{0:T(1024)}, f32[640]{0:T(1024)S(1)}, u32[]{:S(2)}) copy-start(f32[640]{0:T(1024)S(1)} %fusion.66) | copy-start | bytes 7684
  381.3 64.5 %all-to-all-start = ((bf16[1,640,3,1024]{1,2,0,3:T(4,128)(2,1)}), bf16[1,640,3,1024]{1,2,0,3:T(4,128)(2,1)}, u32[]{:S(2)}, u32[]{:S(2)}) async-start(bf16[1,640,3,1024]{1,2,0,3:T(4,128)(2,1)} %pad_maximum_fusion.1), calls=%async_computation | async-start | bytes 10485760 | tf_op jit(solution)/shard_map/all_to_all | solution.py:173
  386.4 254.9 %all-gather.11.cloned.1.call-start = ((), (), s32[]{:S(2)}) async-start(), calls=%async_computation.10 | async-start | bytes 6045696 | tf_op jit(solution)/shard_map/all_gather | solution.py:155
  580.2 7.2 copy-start.39
  583.8 30.6 %all-to-all-start.1 = ((bf16[4,2,81920]{2,1,0:T(2,128)(2,1)}), bf16[4,2,81920]{2,1,0:T(2,128)(2,1)S(1)}, u32[]{:S(2)}, u32[]{:S(2)}) async-start(bf16[4,2,81920]{2,1,0:T(2,128)(2,1)} %reshape.443), calls=%async_computation.1 | async-start | bytes 2621440 | tf_op jit(solution)/shard_map/all_to_all | solution.py:175
  587.3 606.2 %reduce-scatter.7.cloned.1.call-start = ((), (), s32[]{:S(2)}) async-start(), calls=%async_computation.13 | async-start | bytes 2359296 | tf_op jit(solution)/shard_map/reduce_scatter | solution.py:231
  614.4 56.6 %copy-start.33 = (f32[8,1,128]{2,1,0:T(1,128)}, f32[8,1,128]{2,1,0:T(1,128)S(1)}, u32[]{:S(2)}) copy-start(f32[8,1,128]{2,1,0:T(1,128)S(1)} %convert_element_type.214) | copy-start | bytes 12292
  617.1 3.5 copy-start.4
  624.3 1.5 copy-start.7
  624.3 46.7 %copy-start.23 = (f32[640]{0:T(1024)}, f32[640]{0:T(1024)S(1)}, u32[]{:S(2)}) copy-start(f32[640]{0:T(1024)S(1)} %broadcast_multiply_fusion.1) | copy-start | bytes 7684
  626.2 44.9 %copy-start.35 = (f32[640]{0:T(1024)}, f32[640]{0:T(1024)S(1)}, u32[]{:S(2)}) copy-start(f32[640]{0:T(1024)S(1)} %fusion.67) | copy-start | bytes 7684
  641.3 15.2 copy-start.8
  656.4 14.6 copy-start.42
  671.1 1.3 copy-start.11
  672.0 1.5 copy-start.1
  672.0 1.5 copy-start.31
  672.4 1.8 copy-start.19
  674.2 3.2 copy-start.40
  695.1 8.2 copy-start.12
  698.9 21.6 %all-to-all-start.2 = ((bf16[4,2,81920]{2,1,0:T(2,128)(2,1)}), bf16[4,2,81920]{2,1,0:T(2,128)(2,1)}, u32[]{:S(2)}, u32[]{:S(2)}) async-start(bf16[4,2,81920]{2,1,0:T(2,128)(2,1)} %reshape.445), calls=%async_computation.2 | async-start | bytes 2621440 | tf_op jit(solution)/shard_map/all_to_all | solution.py:209
  703.2 490.4 %reduce-scatter.11.cloned.1.call-start = ((), (), s32[]{:S(2)}) async-start(), calls=%async_computation.15 | async-start | bytes 6045696 | tf_op jit(solution)/shard_map/reduce_scatter | solution.py:237
  711.5 569.7 %reduce-scatter.5.cloned.1.call-start = ((), (), s32[]{:S(2)}) async-start(), calls=%async_computation.12 | async-start | bytes 7077888 | tf_op jit(solution)/shard_map/reduce_scatter | solution.py:228
  1050.6 7.7 copy-start
  1058.5 2.1 copy-start.10
  1148.2 2.1 copy-start.17
  1148.2 5.5 slice-start
  1150.2 3.9 slice-start.1
  1153.3 1.1 copy-start.15
  1155.5 2.4 copy-start.5
  1155.5 2.4 copy-start.22
  1155.5 2.4 copy-start.28
  1155.6 2.4 copy-start.30
  1156.0 2.0 copy-start.13
  1165.7 0.7 copy-start.24
  1165.7 0.7 copy-start.34
  1165.7 0.7 copy-start.36
  1165.7 300.4 %reduce-scatter.9.cloned.1.call-start = ((), (), s32[]{:S(2)}) async-start(), calls=%async_computation.14 | async-start | bytes 12091392 | tf_op jit(solution)/shard_map/reduce_scatter | solution.py:234
  1182.1 0.8 copy-start.41
  1182.1 384.4 %all-gather.13.cloned.1.call-start = ((), (), s32[]{:S(2)}) async-start(), calls=%async_computation.11 | async-start | bytes 7077888 | tf_op jit(solution)/shard_map/all_gather | solution.py:190
  1182.8 452.4 %all-reduce.9.cloned.1.call-start = ((), (), s32[]{:S(2)}) async-start(), calls=%async_computation.16 | async-start | bytes 6127616 | tf_op jit(solution)/shard_map/psum | solution.py:244
  1466.2 108.5 %copy-start.26 = (f32[640]{0:T(1024)S(1)}, f32[640]{0:T(1024)}, u32[]{:S(2)}) copy-start(f32[640]{0:T(1024)} %copy-done.25) | copy-start | bytes 7684
  1566.5 8.2 copy-start.6
  1574.6 1.5 copy-start.9
  1574.6 1.5 copy-start.37
  1574.6 27.4 %copy-start.2 = (f32[640,1024]{1,0:T(8,128)S(1)}, f32[640,1024]{1,0:T(8,128)}, u32[]{:S(2)}) copy-start(f32[640,1024]{1,0:T(8,128)} %copy-done.1) | copy-start | bytes 7864324
  1574.7 27.4 %copy-start.32 = (f32[640]{0:T(1024)S(1)}, f32[640]{0:T(1024)}, u32[]{:S(2)}) copy-start(f32[640]{0:T(1024)} %copy-done.31) | copy-start | bytes 7684
  1635.3 4.4 copy-start.20
  1635.3 5.6 copy-start.18
Sparse Core Ops, SparseCore 0:
  10.1 65.7 all-gather.6
  78.1 281.2 all-gather.8
  389.4 96.5 all-gather.10
  677.5 65.5 reduce-scatter.6
  746.6 103.3 reduce-scatter.10
  1165.9 115.3 reduce-scatter.4
  1285.3 180.8 reduce-scatter.8
  1468.3 98.1 all-gather.12
  1569.1 66.0 all-reduce.8
